TPU v7x, 128 devices: a whole 4x4x4 slice. The times are simulated.
128 devices in a mesh: seq: 16 (over z, y_hi, core), col: 4 (over x), batch: 2 (over y_lo).
Axes of the slice: x: 4, y: 4 (y_hi: 2, y_lo: 2; y = y_hi * 2 + y_lo), z: 4, core: 2. Of those that a mesh axis runs over, the one named last changes fastest.
Arguments:
- tokens: int32 [2, 1048576], P('batch', ('seq', 'col')), may hold values from 0 to 3
- stem_weight: bfloat16 [64, 768], replicated, may hold values from -1.5 to 1.5
- conv_weight: bfloat16 [3840, 768], replicated, may hold values from -0.09375 to 0.09375
- conv_bias: float32 [768], replicated, may hold values from -1 to 1
- up_weight: bfloat16 [768, 1536], replicated, may hold values from -0.21875 to 0.21875
- norm_gain: float32 [1536], replicated, may hold values from 0.1 to 1.9
- pair_weight: bfloat16 [1536, 64], replicated, may hold values from -0.15625 to 0.15625
- out_weight: bfloat16 [1024, 128], replicated, may hold values from -0.1875 to 0.1875
- cotangent: bfloat16 [2, 512, 512, 128], P('batch', 'seq', 'col'), may hold values from -24 to 24
- projection: float32 [768, 128], replicated, may hold values from -0.21875 to 0.21875
- buckets: int32 [3840], replicated, may hold values from 0 to 31
Outputs:
- input_grad: bfloat16 [2, 65536, 768], P('batch', ('seq', 'col'))
- embedding: float32 [2, 32, 128], P('batch')
All inputs are finite; a program needn't handle non-finite values.
Results may differ from a plain program's by a relative error of at most 0.012.
Values may be sent and summed in bfloat16 or wider, within the bound.
No kernel may reach another device: no remote copies, remote signals or barrier semaphores. Data moves between devices by JAX's collectives and lax.ppermute only.
A program may use at most 128 MiB of HBM per device.

v0:
```python
import jax
import jax.numpy as jnp
from jax import lax
from jax.sharding import PartitionSpec as P

OP = 32
PATCH = 16
POOL = 128
BUCKETS = 32
highest = lax.Precision.HIGHEST


def extended(cells, sides, width):
    for axis, dim in sides:
        count = lax.axis_size(axis)
        ends = count - 1
        head = lax.slice_in_dim(cells, 0, width, axis=dim)
        tail = lax.slice_in_dim(cells, cells.shape[dim] - width, cells.shape[dim], axis=dim)
        cells = jnp.concatenate(
            [
                lax.ppermute(tail, axis, [(i, (i + 1) % count) for i in range(ends)]),
                cells,
                lax.ppermute(head, axis, [((i + 1) % count, i) for i in range(ends)]),
            ],
            axis=dim,
        )
    return cells


def shards(
    tokens,
    stem_weight,
    conv_weight,
    conv_bias,
    up_weight,
    norm_gain,
    pair_weight,
    out_weight,
    cotangent,
    projection,
    buckets,
):
    channels = conv_weight.shape[1]
    kernel = conv_weight.shape[0] // channels
    reach = (kernel - 1) // 2
    patches = tokens.shape[1] // PATCH
    bins_dev = patches // POOL
    bases = tokens[0].reshape(patches, PATCH)
    onehot = (
        (bases[:, :, None] == jnp.arange(4, dtype=jnp.int32))
        .astype(jnp.bfloat16)
        .reshape(patches, PATCH * 4)
    )
    embedded = jnp.dot(onehot, stem_weight, preferred_element_type=jnp.float32).astype(jnp.bfloat16)
    padded = extended(embedded, ((("seq", "col"), 0),), reach)
    unfolded = jnp.concatenate(
        [padded[offset : offset + patches] for offset in range(kernel)], axis=1
    )
    before = jnp.dot(unfolded, conv_weight, preferred_element_type=jnp.float32) + conv_bias
    after, gelu_back = jax.vjp(jax.nn.gelu, before)
    pooled = jnp.mean(after.reshape(bins_dev, POOL, channels), axis=1).astype(jnp.bfloat16)
    hidden = jnp.dot(pooled, up_weight, preferred_element_type=jnp.float32)
    inverse = lax.rsqrt(jnp.mean(hidden * hidden, axis=1, keepdims=True) + 1e-06)
    normed = (hidden * inverse * norm_gain).astype(jnp.bfloat16)
    seq_count = lax.axis_size("seq")
    col_count = lax.axis_size("col")
    row_len = bins_dev * col_count
    col_len = bins_dev * seq_count
    all_bins = row_len * seq_count
    row_index = lax.axis_index("seq")
    col_index = lax.axis_index("col")
    every = lax.all_gather(normed, ("seq", "col"), axis=0, tiled=True)
    row_part = lax.dynamic_slice_in_dim(every, row_index * row_len, row_len, 0)
    col_part = lax.dynamic_slice_in_dim(every, col_index * col_len, col_len, 0)
    left = jnp.dot(row_part, pair_weight[:, :OP], preferred_element_type=jnp.float32).astype(
        jnp.bfloat16
    )
    right = jnp.dot(col_part, pair_weight[:, OP:], preferred_element_type=jnp.float32).astype(
        jnp.bfloat16
    )
    pair_channels = cotangent.shape[3]
    blocks = cotangent[0].reshape(col_count, bins_dev, col_len, pair_channels)
    left_groups = left.astype(jnp.float32).reshape(col_count, bins_dev, OP)
    right_wide = right.astype(jnp.float32)

    def pair_step(carry, inputs):
        block, rows_left = inputs
        outer_grad = lax.dot_general(
            block.reshape(bins_dev * col_len, pair_channels),
            out_weight,
            (((1,), (1,)), ((), ())),
            preferred_element_type=jnp.float32,
        ).reshape(bins_dev, col_len, OP, OP)
        grad_left = jnp.einsum("ijkl,jl->ik", outer_grad, right_wide, precision=highest)
        carry = carry + jnp.einsum("ijkl,ik->jl", outer_grad, rows_left, precision=highest)
        return (carry, grad_left)

    grad_right, grad_left = lax.scan(
        pair_step, jnp.zeros((col_len, OP), jnp.float32), (blocks, left_groups)
    )
    grad_left = grad_left.reshape(row_len, OP)
    row_term = lax.dot_general(
        grad_left,
        pair_weight[:, :OP].astype(jnp.float32),
        (((1,), (1,)), ((), ())),
        precision=highest,
    )
    col_term = lax.dot_general(
        grad_right,
        pair_weight[:, OP:].astype(jnp.float32),
        (((1,), (1,)), ((), ())),
        precision=highest,
    )
    empty_rows = jnp.zeros((all_bins, row_term.shape[1]), jnp.float32)
    placed = lax.dynamic_update_slice_in_dim(
        empty_rows, row_term, row_index * row_len, 0
    ) + lax.dynamic_update_slice_in_dim(empty_rows, col_term, col_index * col_len, 0)
    d_normed = lax.psum_scatter(placed, ("seq", "col"), scatter_dimension=0, tiled=True)
    scaled = d_normed * norm_gain
    inner = jnp.mean(scaled * hidden, axis=1, keepdims=True)
    d_hidden = inverse * scaled - hidden * inverse**3 * inner
    d_pooled = lax.dot_general(
        d_hidden, up_weight.astype(jnp.float32), (((1,), (1,)), ((), ())), precision=highest
    )
    spread = jnp.broadcast_to(d_pooled[:, None, :] / POOL, (bins_dev, POOL, channels)).reshape(
        patches, channels
    )
    d_before = gelu_back(spread)[0].astype(jnp.bfloat16)
    grads_padded = extended(d_before, ((("seq", "col"), 0),), reach)
    stacked = jnp.stack(
        [
            grads_padded[2 * reach - offset : 2 * reach - offset + patches]
            for offset in range(kernel)
        ],
        axis=1,
    )
    input_grad = jnp.einsum(
        "tko,kio->ti",
        stacked,
        conv_weight.reshape(kernel, channels, channels),
        preferred_element_type=jnp.float32,
    ).astype(jnp.bfloat16)
    share_rows = unfolded.shape[1] // lax.axis_size(("seq", "col"))
    share = lax.psum_scatter(
        lax.dot_general(
            unfolded, d_before, (((0,), (0,)), ((), ())), preferred_element_type=jnp.float32
        ),
        ("seq", "col"),
        scatter_dimension=0,
        tiled=True,
    )
    labels = lax.dynamic_slice_in_dim(
        buckets, lax.axis_index(("seq", "col")) * share_rows, share_rows, 0
    )
    projected = jnp.dot(share, projection, precision=highest)
    member = (labels[None, :] == jnp.arange(BUCKETS, dtype=jnp.int32)[:, None]).astype(jnp.float32)
    sketch = lax.psum(jnp.dot(member, projected, precision=highest), ("seq", "col"))
    unit = sketch * lax.rsqrt(jnp.mean(sketch * sketch) + 1e-06)
    center = lax.psum(unit, "batch") / lax.axis_size("batch")
    return (input_grad[None], (unit - center)[None])


def solution(mesh):
    in_specs = (
        P("batch", ("seq", "col")),
        P(),
        P(),
        P(),
        P(),
        P(),
        P(),
        P(),
        P("batch", "seq", "col", None),
        P(),
        P(),
    )
    out_specs = (P("batch", ("seq", "col"), None), P("batch", None, None))
    return jax.shard_map(shards, mesh=mesh, in_specs=in_specs, out_specs=out_specs, check_vma=False)
```

profile of v0, /device:TPU:8, one launch (start us, length us, event | category | flops | bytes accessed | tf_op | source)
XLA Modules:
  0.0 925.7 jit_solution(1880735338173199356)
XLA Ops:
  7.2 0.5 broadcast.83
  7.7 1.8 reduce.3
  9.5 0.2 eq.35
  9.7 0.2 copy.16
  10.2 1.6 convolution_convert_fusion
  11.8 3.4 collective-permute-start
  15.2 1.3 collective-permute-start.1
  16.5 0.4 fusion.29
  16.9 0.4 fusion.35
  17.4 3.3 collective-permute-done.1
  20.7 0.4 fusion.27
  21.0 0.4 fusion.34
  21.5 8.4 bitcast_reduce_fusion
  29.9 0.5 multiply_reduce_fusion.1
  30.4 0.7 multiply_convert_fusion
  31.2 0.2 reduce-scatter.4.cloned.1.call-start
  31.4 72.0 %all-gather.2.cloned.1.call-done = bf16[512,1536]{1,0:T(8,128)(2,1)} async-done(((bf16[8,1536]{1,0:T(8,128)(2,1)}), bf16[512,1536]{1,0:T(8,128)(2,1)}) %all-gather.2.cloned.1.call-update) | async-done | bytes 1572880 | tf_op jit(solution)/shard_map/all_gather | solution.py:72
  103.4 1.2 fusion.37
  104.8 1.0 fusion.39
  105.8 78.4 %while.13 = (s32[]{:T(128)}, f32[128,32]{1,0:T(8,128)S(1)}, f32[4,8,32]{2,1,0:T(8,128)S(1)}, bf16[4,8,128,128]{3,2,1,0:T(8,128)(2,1)}, bf16[1024,128]{1,0:T(8,12...) while((s32[]{:T(128)}, f32[128,32]{1,0:T(8,128)S(1)}, ...), condition=%wide.region_3.4_spmd.clone, body=%wide.region_2.3_spmd.clone.sunk | while | flops 293609472 | bytes 30050948 | solution.py:98
  105.8 3.6 fusion.101
  109.5 11.1 %fusion.102 = f32[1,8,32,1]{2,0,3,1:T(1,128)S(1)} fusion(f32[128,32,1,1]{0,2,1,3:T(1,128)S(1)} %copy.35, f32[8,128,32,32]{1,3,2,0:T(8,128)} %fusion.101), kind=kOutput, calls=%fused_computation.clone.1 | convolution fusion | flops 12582912 | bytes 4211712 | tf_op jit(solution)/shard_map/while/body/eval_jaxpr/ijkl,jl->ik/dot_general | solution.py:94
  120.6 4.7 fusion.103
  125.4 3.6 fusion.101
  129.1 11.1 %fusion.102 = f32[1,8,32,1]{2,0,3,1:T(1,128)S(1)} fusion(f32[128,32,1,1]{0,2,1,3:T(1,128)S(1)} %copy.35, f32[8,128,32,32]{1,3,2,0:T(8,128)} %fusion.101), kind=kOutput, calls=%fused_computation.clone.1 | convolution fusion | flops 12582912 | bytes 4211712 | tf_op jit(solution)/shard_map/while/body/eval_jaxpr/ijkl,jl->ik/dot_general | solution.py:94
  140.2 4.7 fusion.103
  145.0 3.6 fusion.101
  148.7 11.1 %fusion.102 = f32[1,8,32,1]{2,0,3,1:T(1,128)S(1)} fusion(f32[128,32,1,1]{0,2,1,3:T(1,128)S(1)} %copy.35, f32[8,128,32,32]{1,3,2,0:T(8,128)} %fusion.101), kind=kOutput, calls=%fused_computation.clone.1 | convolution fusion | flops 12582912 | bytes 4211712 | tf_op jit(solution)/shard_map/while/body/eval_jaxpr/ijkl,jl->ik/dot_general | solution.py:94
  159.8 4.7 fusion.103
  164.6 3.6 fusion.101
  168.3 11.1 %fusion.102 = f32[1,8,32,1]{2,0,3,1:T(1,128)S(1)} fusion(f32[128,32,1,1]{0,2,1,3:T(1,128)S(1)} %copy.35, f32[8,128,32,32]{1,3,2,0:T(8,128)} %fusion.101), kind=kOutput, calls=%fused_computation.clone.1 | convolution fusion | flops 12582912 | bytes 4211712 | tf_op jit(solution)/shard_map/while/body/eval_jaxpr/ijkl,jl->ik/dot_general | solution.py:94
  179.4 4.7 fusion.103
  184.2 2.0 broadcast_in_dim.16
  186.2 0.9 convolution_dynamic-update-slice_fusion
  187.1 2.5 fusion.19
  189.7 0.6 dynamic-slice.5
  190.9 0.8 dynamic_slice.19
  191.7 143.6 %reduce-scatter.4.cloned.1.call-done = f32[8,1536]{1,0:T(8,128)} async-done(((f32[512,1536]{1,0:T(8,128)}), f32[8,1536]{1,0:T(8,128)}) %reduce-scatter.4.cloned.1.call-update) | async-done | bytes 49168 | tf_op jit(solution)/shard_map/reduce_scatter | solution.py:118
  335.3 0.9 multiply_reduce_fusion
  336.2 2.7 convolution_multiply_fusion
  339.0 3.7 fusion.15
  342.7 12.6 %fusion.70 = f32[3840,768]{1,0:T(8,128)} fusion(bf16[1024,3840]{1,0:T(8,128)(2,1)} %copy-done.6, bf16[1024,768]{1,0:T(8,128)(2,1)S(1)} %fusion.15), kind=kOutput, calls=%fused_computation.110 | convolution fusion | flops 6039797760 | bytes 21233664 | tf_op jit(solution)/shard_map/dot_general | solution.py:145
  355.3 1.3 collective-permute-start.2
  356.6 201.8 %fusion = f32[64,768]{1,0:T(8,128)S(1)} fusion(f32[3840,768]{1,0:T(8,128)} %fusion.70), kind=kCustom, calls=%all-reduce-scatter | all-reduce-scatter fusion | flops 3145729 | bytes 11993600
  558.4 1.4 collective-permute-start.4
  559.8 1.3 collective-permute-start.5
  561.1 2.0 collective-permute-start.6
  563.1 1.3 collective-permute-start.7
  564.4 1.3 collective-permute-start.3
  565.8 1.9 fusion.25
  567.7 0.4 fusion.33
  568.2 0.4 fusion.22
  568.6 0.4 fusion.31
  569.0 0.6 slice-done.3
  569.6 7.4 fusion.36
  577.0 0.7 copy-done.9
  577.7 0.7 copy-done.8
  578.4 4.3 concatenate.26
  582.7 1.4 fusion.42
  584.1 0.1 fusion.60
  584.2 323.5 %psum.14 = f32[32,128]{1,0:T(8,128)S(1)} all-reduce(f32[32,128]{1,0:T(8,128)S(1)} %fusion.60), channel_id=1, replica_groups=mesh['seq'=16,'col'=4,'batch'=2] {'seq','col'}, use_global_device_ids=true, to_apply=%region_7.8 | all-reduce | flops 4096 | bytes 32768 | tf_op jit(solution)/shard_map/psum | solution.py:157
  907.7 0.6 multiply_reduce_fusion.2
  909.0 9.2 psum.15
  918.3 0.6 subtract_bitcast_fusion
  (80 shorter events, 1.6 us)
Async XLA Ops:
  7.2 22.7 %copy-start = (bf16[768,1536]{1,0:T(8,128)(2,1)S(1)}, bf16[768,1536]{1,0:T(8,128)(2,1)}, u32[]{:S(2)}) copy-start(bf16[768,1536]{1,0:T(8,128)(2,1)} %param.17) | copy-start | bytes 7077892
  7.2 96.2 %all-gather.2.cloned.1.call-start = ((), (), s32[]{:S(2)}) async-start(), calls=%async_computation.1 | async-start | bytes 1597440 | tf_op jit(solution)/shard_map/all_gather | solution.py:72
  11.8 4.7 collective-permute-start
  15.2 5.5 collective-permute-start.1
  16.5 4.9 slice-start
  17.3 4.2 slice-start.1
  17.4 4.1 copy-start.11
  21.5 8.4 copy-start.6
  21.5 9.0 copy-start.10
  21.5 81.9 %copy-start.5 = (bf16[1536,64]{0,1:T(8,128)(2,1)S(1)}, bf16[1536,64]{0,1:T(8,128)(2,1)}, u32[]{:S(2)}) copy-start(bf16[1536,64]{0,1:T(8,128)(2,1)} %param.19) | copy-start | bytes 589828
  29.9 75.9 %copy-start.4 = (bf16[1024,128]{1,0:T(8,128)(2,1)S(1)}, bf16[1024,128]{1,0:T(8,128)(2,1)}, u32[]{:S(2)}) copy-start(bf16[1024,128]{1,0:T(8,128)(2,1)} %param.20) | copy-start | bytes 786436
  31.2 304.1 %reduce-scatter.4.cloned.1.call-start = ((), (), s32[]{:S(2)}) async-start(), calls=%async_computation.2 | async-start | bytes 3194880 | tf_op jit(solution)/shard_map/reduce_scatter | solution.py:118
  109.5 11.1 %copy-start.1 = (f32[8,128,32,32]{1,3,2,0:T(8,128)S(1)}, f32[8,128,32,32]{1,3,2,0:T(8,128)}, u32[]{:S(2)}) copy-start(f32[8,128,32,32]{1,3,2,0:T(8,128)} %fusion.101) | copy-start | bytes 12582916 | tf_op jit(solution)/shard_map/while
  129.1 11.1 %copy-start.1 = (f32[8,128,32,32]{1,3,2,0:T(8,128)S(1)}, f32[8,128,32,32]{1,3,2,0:T(8,128)}, u32[]{:S(2)}) copy-start(f32[8,128,32,32]{1,3,2,0:T(8,128)} %fusion.101) | copy-start | bytes 12582916 | tf_op jit(solution)/shard_map/while
  148.7 11.1 %copy-start.1 = (f32[8,128,32,32]{1,3,2,0:T(8,128)S(1)}, f32[8,128,32,32]{1,3,2,0:T(8,128)}, u32[]{:S(2)}) copy-start(f32[8,128,32,32]{1,3,2,0:T(8,128)} %fusion.101) | copy-start | bytes 12582916 | tf_op jit(solution)/shard_map/while
  168.3 11.1 %copy-start.1 = (f32[8,128,32,32]{1,3,2,0:T(8,128)S(1)}, f32[8,128,32,32]{1,3,2,0:T(8,128)}, u32[]{:S(2)}) copy-start(f32[8,128,32,32]{1,3,2,0:T(8,128)} %fusion.101) | copy-start | bytes 12582916 | tf_op jit(solution)/shard_map/while
  186.2 3.4 copy-start.12
  342.7 12.6 %copy-start.2 = (bf16[1024,768]{1,0:T(8,128)(2,1)}, bf16[1024,768]{1,0:T(8,128)(2,1)S(1)}, u32[]{:S(2)}) copy-start(bf16[1024,768]{1,0:T(8,128)(2,1)S(1)} %fusion.15) | copy-start | bytes 4718596
  355.3 209.1 %collective-permute-start.2 = (bf16[2,768]{1,0:T(2,128)(2,1)S(1)}, bf16[2,768]{1,0:T(2,128)(2,1)S(1)}, u32[]{:S(2)}, u32[]{:S(2)}) collective-permute-start(bf16[2,768]{1,0:T(2,128)(2,1)S(1)} %get-tuple-element.104), channel_id=1, source_target_pairs={{2,0},{4,2},{6,4},{8,6},{10,8},{12,10},{14,12},{16,14},{18,16},{20... | collective-permute-start | bytes 9224 | tf_op jit(solution)/shard_map/ppermute | solution.py:23
  558.3 9.3 %copy-start.3 = (bf16[1024,768]{1,0:T(8,128)(2,1)S(1)}, bf16[1024,768]{1,0:T(8,128)(2,1)}, u32[]{:S(2)}) copy-start(bf16[1024,768]{1,0:T(8,128)(2,1)} %copy-done.2) | copy-start | bytes 4718596
  558.4 18.6 %collective-permute-start.4 = (f32[64,768]{1,0:T(8,128)S(1)}, f32[64,768]{1,0:T(8,128)S(1)}, u32[]{:S(2)}, u32[]{:S(2)}) collective-permute-start(f32[64,768]{1,0:T(8,128)S(1)} %fusion), channel_id=1, source_target_pairs={{0,2},{2,4},{4,6},{6,8},{8,10},{10,12},{12,14},{14,16},{16,18},{18... | collective-permute-start | bytes 589832
  559.8 17.2 %collective-permute-start.5 = (f32[64,768]{1,0:T(8,128)S(1)}, f32[64,768]{1,0:T(8,128)S(1)}, u32[]{:S(2)}, u32[]{:S(2)}) collective-permute-start(f32[64,768]{1,0:T(8,128)S(1)} %fusion), channel_id=1, source_target_pairs={{0,4},{2,6},{4,8},{6,10},{8,12},{10,14},{12,16},{14,18},{16,20},{1... | collective-permute-start | bytes 589832
  561.1 17.3 %collective-permute-start.6 = (f32[64,768]{1,0:T(8,128)S(1)}, f32[64,768]{1,0:T(8,128)}, u32[]{:S(2)}, u32[]{:S(2)}) collective-permute-start(f32[64,768]{1,0:T(8,128)S(1)} %fusion), channel_id=1, source_target_pairs={{0,6},{2,8},{4,10},{6,12},{8,14},{10,16},{12,18},{14,20},{16,22},{... | collective-permute-start | bytes 589832
  563.1 13.9 %collective-permute-start.7 = (f32[60,768]{1,0:T(8,128)S(1)}, f32[60,768]{1,0:T(8,128)S(1)}, u32[]{:S(2)}, u32[]{:S(2)}) collective-permute-start(f32[60,768]{1,0:T(8,128)S(1)} %slice.78), channel_id=1, source_target_pairs={{0,8},{2,10},{4,12},{6,14},{8,16},{10,18},{12,20},{14,22},{16,24},... | collective-permute-start | bytes 552968
  564.4 3.8 collective-permute-start.3
  565.7 3.2 slice-start.2
  568.1 1.5 slice-start.3
  577.0 0.7 copy-start.9
  577.0 0.7 copy-start.7
  577.7 0.7 copy-start.8
Sparse Core Ops, SparseCore 0:
  31.3 72.0 all-gather.1
  189.8 145.4 reduce-scatter.3
where the time goes:
time: 927 us; the launch traced here: 926 us
  blocking collectives  535 us (58%)
  waiting for transfers between devices  219 us (24%)
  matrix products  118 us (13%)
  between operations  15.9 us (2%)
  starting transfers between devices  13.6 us (1%)
  other arithmetic  13 us (1%)
  local copies, waits for them, and re-layouts  11.9 us (1%)
    psum x1, blocking collectives, shards(): lax.psum(jnp.dot(member, projected, precision=highest), ('seq', 'col'))  324 us
    unnamed x1, blocking collectives  202 us
    reduce_scatter x1, waiting for transfers between devices, shards(): lax.psum_scatter(placed, ('seq', 'col'), scatter_dimension=0, tiled=True)  144 us
    all_gather x1, waiting for transfers between devices, shards(): every = lax.all_gather(normed, ('seq', 'col'), axis=0, tiled=True)  72 us
    dot_general x4, matrix products, pair_step(): jnp.einsum('ijkl,jl->ik', outer_grad, right_wide, precision=highest)  44.3 us
    dot_general x4, matrix products, pair_step(): jnp.einsum('ijkl,ik->jl', outer_grad, rows_left, precision=highest)  18.7 us
  transfers between devices with their start and end apart: 10, of which 3 were waited for; matrix products, arithmetic and copies ran while one was open for 23% of the time, Pallas kernels for 0%

commit v1 on v0

--- a/solution.py
+++ b/solution.py
@@ -154,7 +154,9 @@
     )
     projected = jnp.dot(share, projection, precision=highest)
     member = (labels[None, :] == jnp.arange(BUCKETS, dtype=jnp.int32)[:, None]).astype(jnp.float32)
-    sketch = lax.psum(jnp.dot(member, projected, precision=highest), ("seq", "col"))
+    sketch = jnp.dot(member, projected, precision=highest)
+    for over in ("seq", "col"):
+        sketch = lax.psum(sketch, over)
     unit = sketch * lax.rsqrt(jnp.mean(sketch * sketch) + 1e-06)
     center = lax.psum(unit, "batch") / lax.axis_size("batch")
     return (input_grad[None], (unit - center)[None])

time: 927 us -> 687 us (0.74)
  blocking collectives: 535 us -> 294 us
    psum x1 -> x2, blocking collectives: 324 us -> 82 us  [shards(): sketch = lax.psum(sketch, over)]
  transfers between devices with their start and end apart: 10 -> 10, of which waited for: 3 -> 3; matrix products, arithmetic and copies ran while one was open for 23% -> 31% of each run, Pallas kernels for 0% -> 0%
where the time goes in v1:
time: 687 us; the launch traced here: 686 us
  blocking collectives  294 us (43%)
  waiting for transfers between devices  219 us (32%)
  matrix products  118 us (17%)
  between operations  15.9 us (2%)
  starting transfers between devices  14.4 us (2%)
  other arithmetic  13 us (2%)
  local copies, waits for them, and re-layouts  11.9 us (2%)
    unnamed x1, blocking collectives  202 us
    reduce_scatter x1, waiting for transfers between devices, shards(): lax.psum_scatter(placed, ('seq', 'col'), scatter_dimension=0, tiled=True)  144 us
    psum x2, blocking collectives, shards(): sketch = lax.psum(sketch, over)  82 us
    all_gather x1, waiting for transfers between devices, shards(): every = lax.all_gather(normed, ('seq', 'col'), axis=0, tiled=True)  72 us
    dot_general x4, matrix products, pair_step(): jnp.einsum('ijkl,jl->ik', outer_grad, right_wide, precision=highest)  44.3 us
    dot_general x4, matrix products, pair_step(): jnp.einsum('ijkl,ik->jl', outer_grad, rows_left, precision=highest)  18.7 us
    dot_general x4, matrix products, pair_step(): lax.dot_general(block.reshape(bins_dev * col_len, pair_channels), out_wei...  14.5 us
  transfers between devices with their start and end apart: 10, of which 3 were waited for; matrix products, arithmetic and copies ran while one was open for 31% of the time, Pallas kernels for 0%

profile of v1, /device:TPU:8, one launch (start us, length us, event | category | flops | bytes accessed | tf_op | source)
XLA Modules:
  0.0 685.5 jit_solution(17896756551876458649)
XLA Ops:
  7.2 0.5 broadcast.83
  7.7 1.8 reduce.3
  9.5 0.2 eq.35
  9.7 0.2 copy.16
  10.2 1.6 convolution_convert_fusion
  11.8 3.4 collective-permute-start
  15.2 1.3 collective-permute-start.1
  16.5 0.4 fusion.29
  16.9 0.4 fusion.35
  17.4 3.3 collective-permute-done.1
  20.7 0.4 fusion.27
  21.0 0.4 fusion.34
  21.5 8.4 %bitcast_reduce_fusion = (f32[8,768]{1,0:T(8,128)S(1)}, f32[1024,768]{1,0:T(8,128)}) fusion(f32[768]{0:T(1024)S(1)} %copy-done.11, bf16[1024,3840]{1,0:T(8,128)(2,1)S(1)} %fusion.34, bf16[3840,768]{1,0:T(8,128)(2,1)S(1)} %bitcast.117), kind=kOutput, calls=%fused_computation.26 | convolution fusion | flops 6047655936 | bytes 16935936 | tf_op jit(solution)/shard_map/dot_general | solution.py:59
  29.9 0.5 multiply_reduce_fusion.1
  30.4 0.7 multiply_convert_fusion
  31.2 0.2 reduce-scatter.4.cloned.1.call-start
  31.4 72.0 %all-gather.2.cloned.1.call-done = bf16[512,1536]{1,0:T(8,128)(2,1)} async-done(((bf16[8,1536]{1,0:T(8,128)(2,1)}), bf16[512,1536]{1,0:T(8,128)(2,1)}) %all-gather.2.cloned.1.call-update) | async-done | bytes 1572880 | tf_op jit(solution)/shard_map/all_gather | solution.py:72
  103.4 1.2 fusion.37
  104.8 1.0 fusion.39
  105.8 78.4 %while.13 = (s32[]{:T(128)}, f32[128,32]{1,0:T(8,128)S(1)}, f32[4,8,32]{2,1,0:T(8,128)S(1)}, bf16[4,8,128,128]{3,2,1,0:T(8,128)(2,1)}, bf16[1024,128]{1,0:T(8,12...) while((s32[]{:T(128)}, f32[128,32]{1,0:T(8,128)S(1)}, ...), condition=%wide.region_3.4_spmd.clone, body=%wide.region_2.3_spmd.clone.sunk | while | flops 293609472 | bytes 30050948 | solution.py:98
  105.8 3.6 fusion.101
  109.5 11.1 %fusion.102 = f32[1,8,32,1]{2,0,3,1:T(1,128)S(1)} fusion(f32[128,32,1,1]{0,2,1,3:T(1,128)S(1)} %copy.35, f32[8,128,32,32]{1,3,2,0:T(8,128)} %fusion.101), kind=kOutput, calls=%fused_computation.clone.1 | convolution fusion | flops 12582912 | bytes 4211712 | tf_op jit(solution)/shard_map/while/body/eval_jaxpr/ijkl,jl->ik/dot_general | solution.py:94
  120.6 4.7 fusion.103
  125.4 3.6 fusion.101
  129.1 11.1 %fusion.102 = f32[1,8,32,1]{2,0,3,1:T(1,128)S(1)} fusion(f32[128,32,1,1]{0,2,1,3:T(1,128)S(1)} %copy.35, f32[8,128,32,32]{1,3,2,0:T(8,128)} %fusion.101), kind=kOutput, calls=%fused_computation.clone.1 | convolution fusion | flops 12582912 | bytes 4211712 | tf_op jit(solution)/shard_map/while/body/eval_jaxpr/ijkl,jl->ik/dot_general | solution.py:94
  140.2 4.7 fusion.103
  145.0 3.6 fusion.101
  148.7 11.1 %fusion.102 = f32[1,8,32,1]{2,0,3,1:T(1,128)S(1)} fusion(f32[128,32,1,1]{0,2,1,3:T(1,128)S(1)} %copy.35, f32[8,128,32,32]{1,3,2,0:T(8,128)} %fusion.101), kind=kOutput, calls=%fused_computation.clone.1 | convolution fusion | flops 12582912 | bytes 4211712 | tf_op jit(solution)/shard_map/while/body/eval_jaxpr/ijkl,jl->ik/dot_general | solution.py:94
  159.8 4.7 fusion.103
  164.6 3.6 fusion.101
  168.3 11.1 %fusion.102 = f32[1,8,32,1]{2,0,3,1:T(1,128)S(1)} fusion(f32[128,32,1,1]{0,2,1,3:T(1,128)S(1)} %copy.35, f32[8,128,32,32]{1,3,2,0:T(8,128)} %fusion.101), kind=kOutput, calls=%fused_computation.clone.1 | convolution fusion | flops 12582912 | bytes 4211712 | tf_op jit(solution)/shard_map/while/body/eval_jaxpr/ijkl,jl->ik/dot_general | solution.py:94
  179.4 4.7 fusion.103
  184.2 2.0 broadcast_in_dim.16
  186.2 0.9 convolution_dynamic-update-slice_fusion
  187.1 2.5 fusion.19
  189.6 0.6 dynamic-slice.5
  190.9 0.8 dynamic_slice.19
  191.6 143.6 %reduce-scatter.4.cloned.1.call-done = f32[8,1536]{1,0:T(8,128)} async-done(((f32[512,1536]{1,0:T(8,128)}), f32[8,1536]{1,0:T(8,128)}) %reduce-scatter.4.cloned.1.call-update) | async-done | bytes 49168 | tf_op jit(solution)/shard_map/reduce_scatter | solution.py:118
  335.3 0.9 multiply_reduce_fusion
  336.2 2.7 convolution_multiply_fusion
  338.9 3.7 fusion.15
  342.6 12.6 %fusion.70 = f32[3840,768]{1,0:T(8,128)} fusion(bf16[1024,3840]{1,0:T(8,128)(2,1)} %copy-done.6, bf16[1024,768]{1,0:T(8,128)(2,1)S(1)} %fusion.15), kind=kOutput, calls=%fused_computation.110 | convolution fusion | flops 6039797760 | bytes 21233664 | tf_op jit(solution)/shard_map/dot_general | solution.py:145
  355.3 1.3 collective-permute-start.2
  356.6 201.8 %fusion = f32[64,768]{1,0:T(8,128)S(1)} fusion(f32[3840,768]{1,0:T(8,128)} %fusion.70), kind=kCustom, calls=%all-reduce-scatter | all-reduce-scatter fusion | flops 3145729 | bytes 11993600
  558.4 1.7 collective-permute-start.4
  560.0 1.3 collective-permute-start.5
  561.3 2.0 collective-permute-start.6
  563.3 1.3 collective-permute-start.7
  564.6 1.9 collective-permute-start.3
  566.6 1.9 fusion.25
  568.5 0.4 fusion.33
  569.0 0.4 fusion.22
  569.4 0.4 fusion.31
  569.8 0.6 slice-done.3
  570.4 7.4 %fusion.36 = bf16[1,1024,768]{2,1,0:T(8,128)(2,1)} fusion(bf16[1024,5,768]{2,0,1:T(8,128)(2,1)S(1)} %fusion.31, bf16[5,768,768]{2,1,0:T(8,128)(2,1)S(1)} %bitcast.120), kind=kOutput, calls=%fused_computation.61 | convolution fusion | flops 6040584192 | bytes 15335424 | tf_op jit(solution)/shard_map/tko,kio->ti/dot_general | solution.py:137
  577.8 0.7 copy-done.9
  578.5 0.7 copy-done.8
  579.2 4.3 concatenate.26
  583.5 1.4 fusion.42
  585.0 67.7 %psum.21 = f32[32,128]{1,0:T(8,128)S(1)} all-reduce(f32[32,128]{1,0:T(8,128)S(1)} %fusion.60), channel_id=1, replica_groups=mesh['seq'=16,'col'=4,'batch'=2] {'seq'}, use_global_device_ids=true, to_apply=%region_7.8 | all-reduce | flops 4096 | bytes 32768 | tf_op jit(solution)/shard_map/psum | solution.py:159
  652.7 14.3 %psum.22 = f32[32,128]{1,0:T(8,128)S(1)} all-reduce(f32[32,128]{1,0:T(8,128)S(1)} %psum.21), channel_id=1, replica_groups=mesh['seq'=16,'col'=4,'batch'=2] {'col'}, use_global_device_ids=true, to_apply=%region_8.9 | all-reduce | flops 4096 | bytes 32768 | tf_op jit(solution)/shard_map/psum | solution.py:159
  667.0 0.6 multiply_reduce_fusion.2
  668.3 9.7 %psum.23 = f32[32,128]{1,0:T(8,128)S(1)} all-reduce(f32[32,128]{1,0:T(8,128)S(1)} %broadcast_multiply_fusion), channel_id=1, replica_groups=mesh['seq'=16,'col'=4,'batch'=2] {'batch'}, use_global_device_ids=true, to_apply=%region_10.11 | all-reduce | flops 4096 | bytes 32768 | tf_op jit(solution)/shard_map/psum | solution.py:161
  678.0 0.6 subtract_bitcast_fusion
  (81 shorter events, 1.7 us)
Async XLA Ops:
  7.2 22.7 %copy-start = (bf16[768,1536]{1,0:T(8,128)(2,1)S(1)}, bf16[768,1536]{1,0:T(8,128)(2,1)}, u32[]{:S(2)}) copy-start(bf16[768,1536]{1,0:T(8,128)(2,1)} %param.17) | copy-start | bytes 7077892
  7.2 96.2 %all-gather.2.cloned.1.call-start = ((), (), s32[]{:S(2)}) async-start(), calls=%async_computation.1 | async-start | bytes 1597440 | tf_op jit(solution)/shard_map/all_gather | solution.py:72
  11.8 4.7 collective-permute-start
  15.2 5.5 collective-permute-start.1
  16.5 4.9 slice-start
  17.3 4.2 slice-start.1
  17.4 4.1 copy-start.11
  21.5 8.4 %copy-start.6 = (bf16[1024,3840]{1,0:T(8,128)(2,1)}, bf16[1024,3840]{1,0:T(8,128)(2,1)S(1)}, u32[]{:S(2)}) copy-start(bf16[1024,3840]{1,0:T(8,128)(2,1)S(1)} %fusion.34) | copy-start | bytes 23592964
  21.5 9.0 %copy-start.10 = (f32[1536]{0:T(1024)S(1)}, f32[1536]{0:T(1024)}, u32[]{:S(2)}) copy-start(f32[1536]{0:T(1024)} %param.18) | copy-start | bytes 18436
  21.5 81.9 %copy-start.5 = (bf16[1536,64]{0,1:T(8,128)(2,1)S(1)}, bf16[1536,64]{0,1:T(8,128)(2,1)}, u32[]{:S(2)}) copy-start(bf16[1536,64]{0,1:T(8,128)(2,1)} %param.19) | copy-start | bytes 589828
  29.9 75.9 %copy-start.4 = (bf16[1024,128]{1,0:T(8,128)(2,1)S(1)}, bf16[1024,128]{1,0:T(8,128)(2,1)}, u32[]{:S(2)}) copy-start(bf16[1024,128]{1,0:T(8,128)(2,1)} %param.20) | copy-start | bytes 786436
  31.2 304.1 %reduce-scatter.4.cloned.1.call-start = ((), (), s32[]{:S(2)}) async-start(), calls=%async_computation.2 | async-start | bytes 3194880 | tf_op jit(solution)/shard_map/reduce_scatter | solution.py:118
  109.5 11.1 %copy-start.1 = (f32[8,128,32,32]{1,3,2,0:T(8,128)S(1)}, f32[8,128,32,32]{1,3,2,0:T(8,128)}, u32[]{:S(2)}) copy-start(f32[8,128,32,32]{1,3,2,0:T(8,128)} %fusion.101) | copy-start | bytes 12582916 | tf_op jit(solution)/shard_map/while
  129.1 11.1 %copy-start.1 = (f32[8,128,32,32]{1,3,2,0:T(8,128)S(1)}, f32[8,128,32,32]{1,3,2,0:T(8,128)}, u32[]{:S(2)}) copy-start(f32[8,128,32,32]{1,3,2,0:T(8,128)} %fusion.101) | copy-start | bytes 12582916 | tf_op jit(solution)/shard_map/while
  148.7 11.1 %copy-start.1 = (f32[8,128,32,32]{1,3,2,0:T(8,128)S(1)}, f32[8,128,32,32]{1,3,2,0:T(8,128)}, u32[]{:S(2)}) copy-start(f32[8,128,32,32]{1,3,2,0:T(8,128)} %fusion.101) | copy-start | bytes 12582916 | tf_op jit(solution)/shard_map/while
  168.3 11.1 %copy-start.1 = (f32[8,128,32,32]{1,3,2,0:T(8,128)S(1)}, f32[8,128,32,32]{1,3,2,0:T(8,128)}, u32[]{:S(2)}) copy-start(f32[8,128,32,32]{1,3,2,0:T(8,128)} %fusion.101) | copy-start | bytes 12582916 | tf_op jit(solution)/shard_map/while
  186.2 3.4 copy-start.12
  342.6 12.6 %copy-start.2 = (bf16[1024,768]{1,0:T(8,128)(2,1)}, bf16[1024,768]{1,0:T(8,128)(2,1)S(1)}, u32[]{:S(2)}) copy-start(bf16[1024,768]{1,0:T(8,128)(2,1)S(1)} %fusion.15) | copy-start | bytes 4718596
  355.3 209.4 %collective-permute-start.2 = (bf16[2,768]{1,0:T(2,128)(2,1)S(1)}, bf16[2,768]{1,0:T(2,128)(2,1)S(1)}, u32[]{:S(2)}, u32[]{:S(2)}) collective-permute-start(bf16[2,768]{1,0:T(2,128)(2,1)S(1)} %get-tuple-element.104), channel_id=1, source_target_pairs={{2,0},{4,2},{6,4},{8,6},{10,8},{12,10},{14,12},{16,14},{18,16},{20... | collective-permute-start | bytes 9224 | tf_op jit(solution)/shard_map/ppermute | solution.py:23
  558.3 10.2 %copy-start.3 = (bf16[1024,768]{1,0:T(8,128)(2,1)S(1)}, bf16[1024,768]{1,0:T(8,128)(2,1)}, u32[]{:S(2)}) copy-start(bf16[1024,768]{1,0:T(8,128)(2,1)} %copy-done.2) | copy-start | bytes 4718596
  558.4 19.4 %collective-permute-start.4 = (f32[64,768]{1,0:T(8,128)S(1)}, f32[64,768]{1,0:T(8,128)S(1)}, u32[]{:S(2)}, u32[]{:S(2)}) collective-permute-start(f32[64,768]{1,0:T(8,128)S(1)} %fusion), channel_id=1, source_target_pairs={{0,2},{2,4},{4,6},{6,8},{8,10},{10,12},{12,14},{14,16},{16,18},{18... | collective-permute-start | bytes 589832
  560.0 17.8 %collective-permute-start.5 = (f32[64,768]{1,0:T(8,128)S(1)}, f32[64,768]{1,0:T(8,128)S(1)}, u32[]{:S(2)}, u32[]{:S(2)}) collective-permute-start(f32[64,768]{1,0:T(8,128)S(1)} %fusion), channel_id=1, source_target_pairs={{0,4},{2,6},{4,8},{6,10},{8,12},{10,14},{12,16},{14,18},{16,20},{1... | collective-permute-start | bytes 589832
  561.3 17.9 %collective-permute-start.6 = (f32[64,768]{1,0:T(8,128)S(1)}, f32[64,768]{1,0:T(8,128)}, u32[]{:S(2)}, u32[]{:S(2)}) collective-permute-start(f32[64,768]{1,0:T(8,128)S(1)} %fusion), channel_id=1, source_target_pairs={{0,6},{2,8},{4,10},{6,12},{8,14},{10,16},{12,18},{14,20},{16,22},{... | collective-permute-start | bytes 589832
  563.3 14.5 %collective-permute-start.7 = (f32[60,768]{1,0:T(8,128)S(1)}, f32[60,768]{1,0:T(8,128)S(1)}, u32[]{:S(2)}, u32[]{:S(2)}) collective-permute-start(f32[60,768]{1,0:T(8,128)S(1)} %slice.78), channel_id=1, source_target_pairs={{0,8},{2,10},{4,12},{6,14},{8,16},{10,18},{12,20},{14,22},{16,24},... | collective-permute-start | bytes 552968
  564.6 4.4 collective-permute-start.3
  566.5 3.2 slice-start.2
  568.9 1.5 slice-start.3
  577.8 0.7 copy-start.9
  577.8 0.7 copy-start.7
  578.5 0.7 copy-start.8
Sparse Core Ops, SparseCore 0:
  31.3 72.0 all-gather.1
  189.7 145.5 reduce-scatter.3
